TPU v7x, 32 devices: a whole 2x2x4 slice. The times are simulated.
32 devices in a mesh: dp: 4 (over y, core), seq: 8 (over z, x).
Axes of the slice: x: 2, y: 2, z: 4, core: 2. Of those that a mesh axis runs over, the one named last changes fastest.
Arguments:
- queries: bfloat16 [4, 4096, 4096], P('dp', 'seq'), may hold values from -150 to 150
- keys: bfloat16 [4, 4096, 512], P('dp', 'seq'), may hold values from -6 to 6
- values: bfloat16 [4, 4096, 512], P('dp', 'seq'), may hold values from -6 to 6
- grad_out: bfloat16 [4, 4096, 4096], P('dp', 'seq'), may hold values from -6 to 6
- proj_in: bfloat16 [4, 4096, 256], P('dp', 'seq'), may hold values from -6 to 6
- segments: int32 [4, 4096], P('dp'), may hold values from 0 to 63, never falling along the last dimension, each value on 1 to 128 neighbouring positions
Outputs:
- grad_q_proj: float32 [256, 4096], P('dp', 'seq')
- grad_kv_proj: float32 [256, 1024], P('dp', 'seq')
Inputs may be any that keep to these rules, and one draw needn't show every extreme that they name: `segments`: document numbers never fall along a sequence; each document has 1 to 128 tokens, and some document has exactly 128.
All inputs are finite; a program needn't handle non-finite values.
Results may differ from a plain program's by a relative error of at most 0.025.
Values may be sent and summed in bfloat16 or wider, within the bound.
No kernel may reach another device: no remote copies, remote signals or barrier semaphores. Data moves between devices by JAX's collectives and lax.ppermute only.
A program may use at most 128 MiB of HBM per device.

v0:
```python
import jax
import jax.numpy as jnp
from jax import lax
from jax.sharding import PartitionSpec as P

H = 32
KV = 4
HD = 128
RANK = 256
DOC = 128


def shifted_window(blocks, filler):
    previous = jnp.concatenate([jnp.full_like(blocks[:1], filler), blocks[:-1]], axis=0)
    return jnp.concatenate([previous, blocks], axis=1)


def attend(q_heads, k_heads, v_heads, g_heads, segment):
    length = q_heads.shape[0]
    head_count = q_heads.shape[1]
    head_width = q_heads.shape[2]
    block_count = length // DOC
    group_size = min(512 // DOC, block_count)
    scaling = head_width ** (-0.5)

    def to_blocks(array):
        return array.reshape((block_count, DOC) + array.shape[1:])

    def grouped(array):
        return array.reshape((block_count // group_size, group_size) + array.shape[1:])

    seg_query = to_blocks(segment)
    seg_key = shifted_window(seg_query, -1)
    q_block = to_blocks(q_heads)
    g_block = to_blocks(g_heads)
    k_window = shifted_window(to_blocks(k_heads), 0.0)
    v_window = shifted_window(to_blocks(v_heads), 0.0)
    causal = jnp.arange(2 * DOC)[None, :] <= jnp.arange(DOC)[:, None] + DOC

    def one_group(items):
        q_part, g_part, k_part, v_part, sq_part, sk_part = items
        allowed = (sq_part[:, :, None] == sk_part[:, None, :]) & causal[None]
        allowed = allowed[:, None]
        scores = (
            jnp.einsum("nqhd,nkhd->nhqk", q_part, k_part, preferred_element_type=jnp.float32)
            * scaling
        )
        scores = jnp.where(allowed, scores, -1e30)
        probs = jnp.exp(scores - jnp.max(scores, axis=-1, keepdims=True))
        probs = jnp.where(allowed, probs, 0.0)
        probs = probs / jnp.sum(probs, axis=-1, keepdims=True)
        probs_b = probs.astype(jnp.bfloat16)
        attn_out = jnp.einsum(
            "nhqk,nkhd->nqhd", probs_b, v_part, preferred_element_type=jnp.float32
        ).astype(jnp.bfloat16)
        delta = jnp.sum(g_part.astype(jnp.float32) * attn_out.astype(jnp.float32), axis=-1)
        dprobs = jnp.einsum("nqhd,nkhd->nhqk", g_part, v_part, preferred_element_type=jnp.float32)
        dscore = (probs * (dprobs - jnp.transpose(delta, (0, 2, 1))[..., None]) * scaling).astype(
            jnp.bfloat16
        )
        dq_part = jnp.einsum(
            "nhqk,nkhd->nqhd", dscore, k_part, preferred_element_type=jnp.float32
        ).astype(jnp.bfloat16)
        dk_part = jnp.einsum("nhqk,nqhd->nkhd", dscore, q_part, preferred_element_type=jnp.float32)
        dv_part = jnp.einsum("nhqk,nqhd->nkhd", probs_b, g_part, preferred_element_type=jnp.float32)
        return (dq_part, dk_part, dv_part)

    items = tuple(
        (grouped(array) for array in (q_block, g_block, k_window, v_window, seg_query, seg_key))
    )
    dq_all, dk_window, dv_window = lax.map(one_group, items)
    dq_all = dq_all.reshape(length, head_count, head_width)

    def fold_window(window):
        window = window.reshape((block_count, 2 * DOC, head_count, head_width))
        later = jnp.concatenate([window[1:, :DOC], jnp.zeros_like(window[:1, :DOC])], axis=0)
        return (
            (window[:, DOC:] + later).reshape(length, head_count, head_width).astype(jnp.bfloat16)
        )

    return (dq_all, fold_window(dk_window), fold_window(dv_window))


def on_device(queries, keys, values, grad_out, proj_in, segments):
    per_group = H // KV
    own_rows = queries.shape[1]
    q_split = queries.reshape(1, own_rows, H, HD)
    g_split = grad_out.reshape(1, own_rows, H, HD)
    q_heads, g_heads = (
        lax.all_to_all(q_split, "seq", split_axis=2, concat_axis=1, tiled=True),
        lax.all_to_all(g_split, "seq", split_axis=2, concat_axis=1, tiled=True),
    )
    k_split = jnp.repeat(keys.reshape(1, own_rows, KV, HD), per_group, axis=2)
    v_split = jnp.repeat(values.reshape(1, own_rows, KV, HD), per_group, axis=2)
    k_heads, v_heads = (
        lax.all_to_all(k_split, "seq", split_axis=2, concat_axis=1, tiled=True),
        lax.all_to_all(v_split, "seq", split_axis=2, concat_axis=1, tiled=True),
    )
    dq_all, dk_all, dv_all = attend(q_heads[0], k_heads[0], v_heads[0], g_heads[0], segments[0])
    length = dq_all.shape[0]
    head_count = dq_all.shape[1]
    grad_rows = jnp.concatenate(
        [
            dq_all.reshape(length, head_count * HD),
            jnp.stack([dk_all, dv_all], axis=1).reshape(length, 2 * head_count * HD),
        ],
        axis=1,
    )
    total = jnp.einsum(
        "lr,lc->rc",
        lax.all_gather(proj_in, "seq", axis=1, tiled=True)[0],
        grad_rows,
        preferred_element_type=jnp.float32,
    )
    q_term = total[:, : head_count * HD]
    kv_local = total[:, head_count * HD :].reshape(RANK, 2, head_count, HD)
    global_heads = lax.axis_index("seq") * head_count + jnp.arange(head_count)
    owners = ((global_heads // per_group)[:, None] == jnp.arange(KV)[None, :]).astype(jnp.float32)
    kv_term = jnp.einsum(
        "rshd,hg->rsgd", kv_local, owners, precision=lax.Precision.HIGHEST
    ).reshape(RANK, 2 * KV * HD)
    kv_part = lax.psum_scatter(kv_term.astype(jnp.bfloat16), "seq", scatter_dimension=1, tiled=True)
    grad_q_proj, grad_kv_proj = (
        lax.psum_scatter(q_term.astype(jnp.bfloat16), "dp", scatter_dimension=0, tiled=True).astype(
            jnp.float32
        ),
        lax.psum_scatter(kv_part, "dp", scatter_dimension=0, tiled=True).astype(jnp.float32),
    )
    return (grad_q_proj, grad_kv_proj)


def solution(mesh):
    in_specs = (
        P("dp", "seq", None),
        P("dp", "seq", None),
        P("dp", "seq", None),
        P("dp", "seq", None),
        P("dp", "seq", None),
        P("dp", None),
    )
    out_specs = (P("dp", "seq"), P("dp", "seq"))
    return jax.shard_map(
        on_device, mesh=mesh, in_specs=in_specs, out_specs=out_specs, check_vma=False
    )
```

profile of v0, /device:TPU:0, one launch (start us, length us, event | category | flops | bytes accessed | tf_op | source)
XLA Modules:
  0.0 785.5 jit_solution(4936320303926897398)
XLA Ops:
  11.4 7.3 all-to-all-start
  18.6 6.5 copy.89
  25.2 6.4 copy.90
  31.6 80.4 %all-to-all-done = bf16[1,512,32,128]{3,1,0,2:T(8,128)(2,1)} async-done(((bf16[1,512,32,128]{3,1,0,2:T(8,128)(2,1)}), bf16[1,512,32,128]{3,1,0,2:T(8,128)(2,1)}, u32[]{:S(2)}, u32[]{:S(2)}) %all-to-all-start) | async-done | bytes 4194336 | tf_op jit(solution)/shard_map/all_to_all | solution.py:96
  111.9 4.6 all-to-all-start.1
  116.7 92.3 %all-to-all-done.1 = bf16[1,512,32,128]{3,1,0,2:T(8,128)(2,1)} async-done(((bf16[1,512,32,128]{3,1,0,2:T(8,128)(2,1)}), bf16[1,512,32,128]{3,1,0,2:T(8,128)(2,1)}, u32[]{:S(2)}, u32[]{:S(2)}) %all-to-all-start.1) | async-done | bytes 4194336 | tf_op jit(solution)/shard_map/all_to_all | solution.py:90
  211.9 4.6 all-to-all-start.3
  216.5 6.5 copy.91
  223.0 6.4 copy.92
  229.4 79.6 %all-to-all-done.3 = bf16[1,512,32,128]{3,1,0,2:T(8,128)(2,1)} async-done(((bf16[1,512,32,128]{3,1,0,2:T(8,128)(2,1)}), bf16[1,512,32,128]{3,1,0,2:T(8,128)(2,1)}, u32[]{:S(2)}, u32[]{:S(2)}) %all-to-all-start.3) | async-done | bytes 4194336 | tf_op jit(solution)/shard_map/all_to_all | solution.py:97
  309.0 4.6 all-to-all-start.2
  322.3 6.3 pad_maximum_fusion
  328.6 6.0 pad_maximum_fusion.1
  334.6 96.9 %all-to-all-done.2 = bf16[1,512,32,128]{3,1,0,2:T(8,128)(2,1)} async-done(((bf16[1,512,32,128]{3,1,0,2:T(8,128)(2,1)}), bf16[1,512,32,128]{3,1,0,2:T(8,128)(2,1)}, u32[]{:S(2)}, u32[]{:S(2)}) %all-to-all-start.2) | async-done | bytes 4194336 | tf_op jit(solution)/shard_map/all_to_all | solution.py:91
  431.5 185.3 %while.15 = (s32[]{:T(128)}, bf16[8,4,128,4,128]{2,1,0,4,3:T(4,128)(2,1)}, f32[8,4,256,4,128]{4,2,1,0,3:T(8,128)}, f32[8,4,256,4,128]{4,2,1,0,3:T(8,128)}, bf16[...) while((s32[]{:T(128)}, ...), condition=%wide.region_4.5_spmd.clone, body=%wide.region_0.4_spmd.clone.sunk | while | flops 814512384 | bytes 51909304 | solution.py:71
  450.0 4.6 constant_dynamic-update-slice_fusion.3
  473.2 4.6 constant_dynamic-update-slice_fusion.3
  496.3 4.6 constant_dynamic-update-slice_fusion.3
  519.5 4.6 constant_dynamic-update-slice_fusion.3
  542.7 4.6 constant_dynamic-update-slice_fusion.3
  565.8 4.6 constant_dynamic-update-slice_fusion.3
  588.9 4.6 constant_dynamic-update-slice_fusion.3
  612.1 4.6 constant_dynamic-update-slice_fusion.3
  625.3 4.4 fusion.23
  629.7 5.7 fusion.24
  635.4 6.2 pad_maximum_fusion.2
  641.6 11.3 %copy.103 = bf16[4096,2,4,128]{0,3,2,1:T(8,128)(2,1)} copy(bf16[4096,2,4,128]{3,0,2,1:T(8,128)(2,1)} %pad_maximum_fusion.2) | data formatting | bytes 16777216 | tf_op jit(solution)/shard_map/stack | solution.py:105
  652.8 7.8 reshape.126
  660.7 7.8 fusion.25
  674.4 59.8 %reduce-scatter.12.cloned.1.call-done = bf16[128,256]{1,0:T(8,128)(2,1)} async-done(((bf16[1024,256]{1,0:T(8,128)(2,1)}), bf16[128,256]{1,0:T(8,128)(2,1)}) %reduce-scatter.12.cloned.1.call-update) | async-done | bytes 65552
  735.8 20.0 %reduce-scatter.10.cloned.1.call-done = bf16[64,512]{1,0:T(8,128)(2,1)} async-done(((bf16[256,512]{1,0:T(8,128)(2,1)}), bf16[64,512]{1,0:T(8,128)(2,1)}) %reduce-scatter.10.cloned.1.call-update) | async-done | bytes 65552
  757.5 20.2 %reduce-scatter.8.cloned.1.call-done = bf16[64,128]{1,0:T(8,128)(2,1)} async-done(((bf16[256,128]{1,0:T(8,128)(2,1)}), bf16[64,128]{1,0:T(8,128)(2,1)}) %reduce-scatter.8.cloned.1.call-update) | async-done | bytes 16400 | tf_op jit(solution)/shard_map/reduce_scatter | solution.py:127
  (177 shorter events, 182.9 us)
Async XLA Ops:
  11.4 100.6 %all-to-all-start = ((bf16[1,512,32,128]{3,1,0,2:T(8,128)(2,1)}), bf16[1,512,32,128]{3,1,0,2:T(8,128)(2,1)}, u32[]{:S(2)}, u32[]{:S(2)}) async-start(bf16[1,512,32,128]{3,1,0,2:T(8,128)(2,1)} %bitcast.152), calls=%async_computation | async-start | bytes 8388608 | tf_op jit(solution)/shard_map/all_to_all | solution.py:96
  31.6 84.9 %copy-start.1 = (bf16[1,512,512]{2,1,0:T(8,128)(2,1)S(1)}, bf16[1,512,512]{2,1,0:T(8,128)(2,1)}, u32[]{:S(2)}) copy-start(bf16[1,512,512]{2,1,0:T(8,128)(2,1)} %param.10) | copy-start | bytes 1572868
  111.9 97.1 %all-to-all-start.1 = ((bf16[1,512,32,128]{3,1,0,2:T(8,128)(2,1)}), bf16[1,512,32,128]{3,1,0,2:T(8,128)(2,1)}, u32[]{:S(2)}, u32[]{:S(2)}) async-start(bf16[1,512,32,128]{3,1,0,2:T(8,128)(2,1)} %copy.90), calls=%async_computation.1 | async-start | bytes 8388608 | tf_op jit(solution)/shard_map/all_to_all | solution.py:90
  211.9 97.1 %all-to-all-start.3 = ((bf16[1,512,32,128]{3,1,0,2:T(8,128)(2,1)}), bf16[1,512,32,128]{3,1,0,2:T(8,128)(2,1)}, u32[]{:S(2)}, u32[]{:S(2)}) async-start(bf16[1,512,32,128]{3,1,0,2:T(8,128)(2,1)} %bitcast.153), calls=%async_computation.3 | async-start | bytes 8388608 | tf_op jit(solution)/shard_map/all_to_all | solution.py:97
  229.4 85.0 %copy-start.2 = (s32[1,4096]{1,0:T(1,128)S(1)}, s32[1,4096]{1,0:T(1,128)}, u32[]{:S(2)}) copy-start(s32[1,4096]{1,0:T(1,128)} %param.13) | copy-start | bytes 49156
  309.0 122.4 %all-to-all-start.2 = ((bf16[1,512,32,128]{3,1,0,2:T(8,128)(2,1)}), bf16[1,512,32,128]{3,1,0,2:T(8,128)(2,1)}, u32[]{:S(2)}, u32[]{:S(2)}) async-start(bf16[1,512,32,128]{3,1,0,2:T(8,128)(2,1)} %copy.92), calls=%async_computation.2 | async-start | bytes 8388608 | tf_op jit(solution)/shard_map/all_to_all | solution.py:91
  313.6 347.1 %all-gather.2.cloned.1.call-start = ((), (), s32[]{:S(2)}) async-start(), calls=%async_computation.7 | async-start | bytes 2359296 | tf_op jit(solution)/shard_map/all_gather | solution.py:111
  314.4 419.8 %reduce-scatter.12.cloned.1.call-start = ((), (), s32[]{:S(2)}) async-start(), calls=%async_computation.10 | async-start | bytes 589824
  436.4 2.8 copy-start.4
  459.6 2.8 copy-start.4
  482.7 2.8 copy-start.4
  505.9 2.8 copy-start.4
  529.1 2.8 copy-start.4
  552.2 2.8 copy-start.4
  575.4 2.8 copy-start.4
  598.4 2.8 copy-start.4
  668.4 1.1 copy-start
  668.5 1.7 copy-start.3
  672.4 83.4 %reduce-scatter.10.cloned.1.call-start = ((), (), s32[]{:S(2)}) async-start(), calls=%async_computation.9 | async-start | bytes 327680
  674.3 103.3 %reduce-scatter.8.cloned.1.call-start = ((), (), s32[]{:S(2)}) async-start(), calls=%async_computation.8 | async-start | bytes 81920 | tf_op jit(solution)/shard_map/reduce_scatter | solution.py:127
Sparse Core Ops, SparseCore 0:
  316.6 102.1 all-gather.1
  672.5 61.6 reduce-scatter.11
  736.6 19.0 reduce-scatter.9
  758.0 19.5 reduce-scatter.7
where the time goes:
time: 789 us; the launch traced here: 785 us
  waiting for transfers between devices  450 us (57%)
  local copies, waits for them, and re-layouts  163 us (21%)
  matrix products  105 us (13%)
  other arithmetic  32.4 us (4%)
  starting transfers between devices  21.1 us (3%)
  between operations  14 us (2%)
    all_to_all x1, waiting for transfers between devices, on_device(): lax.all_to_all(g_split, 'seq', split_axis=2, concat_axis=1, tiled=True)  96.9 us
    all_to_all x1, waiting for transfers between devices, on_device(): lax.all_to_all(q_split, 'seq', split_axis=2, concat_axis=1, tiled=True)  92.3 us
    unnamed x6, waiting for transfers between devices  80.5 us
    all_to_all x1, waiting for transfers between devices, on_device(): lax.all_to_all(k_split, 'seq', split_axis=2, concat_axis=1, tiled=True)  80.4 us
    all_to_all x1, waiting for transfers between devices, on_device(): lax.all_to_all(v_split, 'seq', split_axis=2, concat_axis=1, tiled=True)  79.6 us
    dynamic_update_slice x32, local copies, waits for them, and re-layouts, attend(): dq_all, dk_window, dv_window = lax.map(one_group, items)  76.3 us
    sub x8, matrix products, one_group(): probs = jnp.exp(scores - jnp.max(scores, axis=-1, keepdims=True))  27.1 us
    dot_general x8, matrix products, one_group(): jnp.einsum('nhqk,nkhd->nqhd', probs_b, v_part, preferred_element_type=jnp...  22.3 us
  transfers between devices with their start and end apart: 8, of which 7 were waited for; matrix products, arithmetic and copies ran while one was open for 36% of the time, Pallas kernels for 0%

commit v1 on v0

v1 whole, which is shorter than its diff:
```python
import functools

import jax
import jax.numpy as jnp
from jax import lax
from jax.experimental import pallas as pl
from jax.experimental.pallas import tpu as pltpu
from jax.sharding import PartitionSpec as P

HD = 128
DOC = 128
NT = (((1,), (1,)), ((), ()))
NN = (((1,), (0,)), ((), ()))


def dot(a, b, dims):
    return lax.dot_general(a, b, dims, preferred_element_type=jnp.float32)


def bits_of(n):
    return n.bit_length() - 1


def stage_bits(dp, seq):
    assert dp == 1 << bits_of(dp) and seq == 1 << bits_of(seq)
    dp_bits = [("dp", b) for b in range(bits_of(dp))]
    seq_bits = [("seq", b) for b in range(bits_of(seq))]
    first, rest = dp_bits[:1], dp_bits[1:2] + seq_bits + dp_bits[2:]
    return [first] + [rest[i : i + 2] for i in range(0, len(rest), 2)]


def place_of(row, s, order):
    at = 0
    for axis, b in order:
        at = at * 2 + (((row >> (b - 1)) if axis == "dp" else (s >> b)) & 1)
    return at


def attention_kernel(blocks, per, kv_heads, dp, seq, order, *refs):
    seg_ref, q_ref, g_ref, k_ref, v_ref, pj_ref, hk_ref, hv_ref, hp_ref = refs[:9]
    keep_ref, send_ref, bias, pt, kt, dqt, dk, dv = refs[9:]
    B = hk_ref.shape[0]
    own = q_ref.shape[0]
    nb = own // B
    R = pj_ref.shape[1]
    f32, bf = jnp.float32, jnp.bfloat16
    scale = HD**-0.5
    to_exp2 = scale * 1.4426950408889634
    key = lax.broadcasted_iota(jnp.int32, (B, B), 0)
    qry = lax.broadcasted_iota(jnp.int32, (B, B), 1)
    cur = key <= qry
    cur2 = jnp.concatenate([cur, cur], axis=1)
    group = pl.program_id(0)
    r = R // dp

    @pl.when(group == 0)
    def _():
        dev = lax.axis_index("seq")
        low = lax.axis_index("dp") % 2
        for n in range(nb + 1):
            rows = (hp_ref[...] if n == 0 else pj_ref[(n - 1) * B : n * B]).astype(f32).T
            rows = rows.reshape(dp // 2, 2, r, B)
            for half in range(2):
                part = jnp.where(low == half, rows[:, 0], rows[:, 1]).reshape(R // 2, B)
                pt[half * (R // 2) : (half + 1) * (R // 2), n * B : (n + 1) * B] = part.astype(bf)
        for n in blocks:
            blk = dev * nb + n
            seg_cur = seg_ref[:, pl.ds(pl.multiple_of(blk * B, B), B)]
            prev = jnp.maximum(blk - 1, 0)
            seg_prev = seg_ref[:, pl.ds(pl.multiple_of(prev * B, B), B)]
            seg_prev = jnp.where(blk > 0, seg_prev, -1)
            cur_c = jnp.broadcast_to(seg_cur, (B, B)).astype(f32)
            prev_c = jnp.broadcast_to(seg_prev, (B, B)).astype(f32)
            key_seg = jnp.where(cur, cur_c.T, prev_c.T)
            bias[n] = jnp.where(key_seg == cur_c, 0.0, -1e30)

    dk[...] = jnp.zeros_like(dk)
    dv[...] = jnp.zeros_like(dv)
    for n in range(nb + 1):
        kt[n] = (hk_ref[...] if n == 0 else k_ref[(n - 1) * B : n * B]).T

    def window(ref, halo, n):
        if n:
            return ref[(n - 1) * B : (n + 1) * B]
        return jnp.concatenate([halo[...], ref[:B]], axis=0)

    def cols(hp):
        return [slice((2 * hp + j) * HD, (2 * hp + j + 1) * HD) for j in range(2)]

    def stack(ref, n, hp):
        return jnp.concatenate([ref[n * B : (n + 1) * B, c] for c in cols(hp)], axis=0)

    def scores(n, hp):
        s2 = dot(window(k_ref, hk_ref, n), stack(q_ref, n, hp), NT)
        d2 = dot(window(v_ref, hv_ref, n), stack(g_ref, n, hp), NT)
        return s2, d2

    def soft(n, hp, s2, d2):
        b2 = jnp.concatenate([bias[n], bias[n]], axis=1)
        s = jnp.where(cur2, s2[B:], s2[:B]) + b2
        d = jnp.where(cur2, d2[B:], d2[:B])
        m = jnp.max(s, axis=0, keepdims=True)
        p = jnp.exp2((s - m) * to_exp2)
        total = jnp.sum(p, axis=0, keepdims=True)
        p = p * (1.0 / total)
        delta = jnp.sum(p * d, axis=0, keepdims=True)
        ds = (p * (d - delta)).astype(bf)
        pb = p.astype(bf)
        z = jnp.zeros_like(pb)
        p2 = jnp.concatenate([jnp.where(cur2, z, pb), jnp.where(cur2, pb, z)], axis=0)
        ds2 = jnp.concatenate([jnp.where(cur2, z, ds), jnp.where(cur2, ds, z)], axis=0)
        return p2, ds2

    def gradients(n, hp, p2, ds2):
        rows = slice(n * B, (n + 2) * B)
        dk[rows] += dot(ds2, stack(q_ref, n, hp), NN)
        dv[rows] += dot(p2, stack(g_ref, n, hp), NN)
        kt2 = jnp.concatenate([kt[n], kt[n + 1]], axis=1)
        dq = dot(kt2, ds2, NN).astype(bf)
        for j, c in enumerate(cols(hp)):
            dqt[c, n * B : (n + 1) * B] = dq[:, j * B : (j + 1) * B]

    steps = [(n, hp) for hp in range(per // 2) for n in blocks]
    ready = scores(*steps[0])
    done = None
    for i, step in enumerate(steps):
        after = scores(*steps[i + 1]) if i + 1 < len(steps) else None
        if done is not None:
            gradients(*done)
        done = step + soft(*step, *ready)
        ready = after
    gradients(*done)

    def store(value, s, lane, width):
        for row in range(dp // 2):
            at = place_of(row, s, order)
            keep_ref[at, :, lane : lane + width] = value[row * r : (row + 1) * r]
            send_ref[at, :, lane : lane + width] = value[R // 2 + row * r : R // 2 + (row + 1) * r]

    lo, hi = blocks[0] * B, (blocks[-1] + 1) * B
    q_width = per * kv_heads * HD // seq
    kv_width = 2 * kv_heads * HD // seq
    tok = pt[:, lo + B : hi + B]
    wide = min(2 * HD, q_width)
    for j in range(0, per * HD, wide):
        value = (dot(tok, dqt[j : j + wide, lo:hi], NT) * scale).astype(bf)
        store(value, group * (per * HD // q_width) + j // q_width, j % q_width, wide)
    tok = pt[:, lo : hi + B]
    for which, ref in enumerate((dk, dv)):
        value = dot(tok, ref[lo : hi + B].astype(bf), NN)
        value = (value * scale if which == 0 else value).astype(bf)
        for j in range(0, HD, kv_width):
            s = which * (seq // 2) + group * (HD // kv_width) + j // kv_width
            store(value[:, j : j + kv_width], s, q_width, kv_width)


def attention(blocks, kv_heads, dp, seq, order, queries, grad_out, keys, values, proj, halo, segments):
    hk, hv, hp = halo
    B = hk.shape[0]
    own, width = queries.shape
    per = width // HD // kv_heads
    nb = own // B
    R = proj.shape[1]
    pieces = dp // 2 * seq
    piece = (pieces, R // dp, width // seq + 2 * kv_heads * HD // seq)
    bf, f32 = jnp.bfloat16, jnp.float32
    whole = lambda i: (0, 0)
    col = lambda i: (0, i)
    call = pl.pallas_call(
        functools.partial(attention_kernel, blocks, per, kv_heads, dp, seq, order),
        grid=(kv_heads,),
        in_specs=[
            pl.BlockSpec(segments.shape, whole),
            pl.BlockSpec((own, per * HD), col),
            pl.BlockSpec((own, per * HD), col),
            pl.BlockSpec((own, HD), col),
            pl.BlockSpec((own, HD), col),
            pl.BlockSpec((own, R), whole),
            pl.BlockSpec((B, HD), col),
            pl.BlockSpec((B, HD), col),
            pl.BlockSpec((B, R), whole),
        ],
        out_specs=[pl.BlockSpec(piece, lambda i: (0, 0, 0))] * 2,
        out_shape=[jax.ShapeDtypeStruct(piece, bf)] * 2,
        scratch_shapes=[
            pltpu.VMEM((nb, B, B), f32),
            pltpu.VMEM((R, own + B), bf),
            pltpu.VMEM((nb + 1, HD, B), bf),
            pltpu.VMEM((per * HD, own), bf),
            pltpu.VMEM((own + B, HD), f32),
            pltpu.VMEM((own + B, HD), f32),
        ],
        name="attention",
    )
    return call(segments, queries, grad_out, keys, values, proj, hk, hv, hp)


def exchange(value, dp, seq, flips):
    dp_flip = sum(1 << b for axis, b in flips if axis == "dp")
    seq_flip = sum(1 << b for axis, b in flips if axis == "seq")
    pairs = [
        (d * seq + s, (d ^ dp_flip) * seq + (s ^ seq_flip)) for d in range(dp) for s in range(seq)
    ]
    return lax.ppermute(value, ("dp", "seq"), pairs)


def scatter_sum(value, dp, seq, bits):
    f32, bf = jnp.float32, jnp.bfloat16
    parts = value.reshape((1 << len(bits), -1) + value.shape[1:])
    mine = 0
    for axis, b in bits:
        mine = mine * 2 + ((lax.axis_index(axis) >> b) & 1)
    total = lax.dynamic_index_in_dim(parts, mine, 0, keepdims=False).astype(f32)
    for flip in range((1 << len(bits)) - 1, 0, -1):
        flips = [bit for i, bit in enumerate(bits) if (flip >> (len(bits) - 1 - i)) & 1]
        sent = lax.dynamic_index_in_dim(parts, mine ^ flip, 0, keepdims=False).astype(bf)
        total = total + exchange(sent, dp, seq, flips).astype(f32)
    return total


def on_device(dp, seq, queries, keys, values, grad_out, proj_in, segments):
    own = queries.shape[1]
    kv_heads = keys.shape[2] // HD
    B = DOC
    nb = own // B
    bf = jnp.bfloat16
    tail = jnp.concatenate([keys[0, own - B :], values[0, own - B :], proj_in[0, own - B :]], axis=1)
    tail = lax.ppermute(tail, "seq", [(i, i + 1) for i in range(seq - 1)])
    kw = keys.shape[2]
    halo = (tail[:, :kw], tail[:, kw : 2 * kw], tail[:, 2 * kw :])
    stages = stage_bits(dp, seq)
    order = [bit for bits in stages[1:] for bit in bits]
    keep, send = attention(
        tuple(range(nb)), kv_heads, dp, seq, order,
        queries[0], grad_out[0], keys[0], values[0], proj_in[0], halo, segments,
    )
    total = keep.astype(jnp.float32) + exchange(send, dp, seq, stages[0]).astype(jnp.float32)
    for bits in stages[1:]:
        total = scatter_sum(total, dp, seq, bits)
    total = total[0]
    q_width = queries.shape[2] // seq
    return total[:, :q_width], total[:, q_width:]


def solution(mesh):
    dp, seq = mesh.shape["dp"], mesh.shape["seq"]
    split = P("dp", "seq", None)
    return jax.shard_map(
        functools.partial(on_device, dp, seq),
        mesh=mesh,
        in_specs=(split,) * 5 + (P("dp", None),),
        out_specs=(P("dp", "seq"), P("dp", "seq")),
        check_vma=False,
    )
```

time: 789 us -> 73.8 us (0.09)
  waiting for transfers between devices: 450 us -> 31.4 us
  local copies, waits for them, and re-layouts: 163 us -> 7.27 us
  matrix products: 105 us -> 0 us
  other arithmetic: 32.4 us -> 3.37 us
  Pallas kernels: 0 us -> 17.5 us
  between operations: 14 us -> 0.71 us
    all_to_all x4 -> x0, waiting for transfers between devices: 349 us -> none  [the longest x1 96.9 us: on_device(): lax.all_to_all(g_split, 'seq', split_axis=2, concat_axis=1, tiled=True)]
    unnamed x6 -> x0, waiting for transfers between devices: 80.5 us -> none
    dot_general x42 -> x0, matrix products: 77.9 us -> none  [the longest x8 22.3 us: one_group(): jnp.einsum('nhqk,nkhd->nqhd', probs_b, v_part, preferred_element_type=jnp...]
    dynamic_update_slice x32 -> x0, local copies, waits for them, and re-layouts: 76.3 us -> none  [attend(): dq_all, dk_window, dv_window = lax.map(one_group, items)]
    ppermute x0 -> x8, waiting for transfers between devices: none -> 31.4 us  [the longest x7 24.4 us: exchange(): return lax.ppermute(value, ('dp', 'seq'), pairs)]
    sub x8 -> x0, matrix products: 27.1 us -> none  [one_group(): probs = jnp.exp(scores - jnp.max(scores, axis=-1, keepdims=True))]
    all_to_all x4 -> x0, starting transfers between devices: 21 us -> none  [the longest x1 7.28 us: on_device(): lax.all_to_all(k_split, 'seq', split_axis=2, concat_axis=1, tiled=True)]
    reduce_scatter x1 -> x0, waiting for transfers between devices: 20.2 us -> none  [on_device(): lax.psum_scatter(kv_part, 'dp', scatter_dimension=0, tiled=True)]
  transfers between devices with their start and end apart: 8 -> 8, of which waited for: 7 -> 7; matrix products, arithmetic and copies ran while one was open for 36% -> 0% of each run, Pallas kernels for 0% -> 0%
where the time goes in v1:
time: 73.8 us; the launch traced here: 73.6 us
  waiting for transfers between devices  31.4 us (43%)
  Pallas kernels  17.5 us (24%)
  starting transfers between devices  13.3 us (18%)
  local copies, waits for them, and re-layouts  7.27 us (10%)
  other arithmetic  3.37 us (5%)
    ppermute x7, waiting for transfers between devices, exchange(): return lax.ppermute(value, ('dp', 'seq'), pairs)  24.4 us
    pallas_call x1, Pallas kernels, attention(): return call(segments, queries, grad_out, keys, values, proj, hk, hv, hp)  17.5 us
    ppermute x7, starting transfers between devices, exchange(): return lax.ppermute(value, ('dp', 'seq'), pairs)  8.46 us
    ppermute x1, waiting for transfers between devices, on_device(): tail = lax.ppermute(tail, 'seq', [(i, i + 1) for i in range(seq - 1)])  6.93 us
    ppermute x1, starting transfers between devices, on_device(): tail = lax.ppermute(tail, 'seq', [(i, i + 1) for i in range(seq - 1)])  4.89 us
    add x1, other arithmetic, on_device(): keep.astype(jnp.float32)  2.01 us
    unnamed x6, local copies, waits for them, and re-layouts  1.79 us
  transfers between devices with their start and end apart: 8, of which 7 were waited for; matrix products, arithmetic and copies ran while one was open for 0% of the time, Pallas kernels for 0%

profile of v1, /device:TPU:0, one launch (start us, length us, event | category | flops | bytes accessed | tf_op | source)
XLA Modules:
  0.0 73.6 jit_solution(2226071155686715270)
XLA Ops:
  0.6 0.8 %slice_bitcast_fusion.2 = bf16[128,256]{1,0:T(8,128)(2,1)S(1)} fusion(bf16[1,512,256]{2,1,0:T(8,128)(2,1)} %param.10), kind=kLoop, calls=%fused_computation.17 | loop fusion | bytes 131072 | tf_op jit(solution)/shard_map/squeeze | solution.py:227
  1.5 1.0 %slice_bitcast_fusion = (bf16[128,512]{1,0:T(8,128)(2,1)S(1)}, bf16[128,512]{1,0:T(8,128)(2,1)S(1)}) fusion(bf16[1,512,512]{2,1,0:T(8,128)(2,1)} %param.8, bf16[1,512,512]{2,1,0:T(8,128)(2,1)} %param.7), kind=kLoop, calls=%fused_computation.15 | loop fusion | bytes 524288 | tf_op jit(solution)/shard_map/squeeze | solution.py:227
  2.5 4.9 %collective-permute-start = (bf16[128,1280]{1,0:T(8,128)(2,1)S(1)}, bf16[128,1280]{1,0:T(8,128)(2,1)S(1)}, u32[]{:S(2)}, u32[]{:S(2)}) collective-permute-start(bf16[128,1280]{1,0:T(8,128)(2,1)S(1)} %pad_maximum_fusion), channel_id=1, source_target_pairs={{0,1},{1,2},{2,3},{3,4},{4,5},{5,6},{6,7},{8,9},{9,10},{10,11},{11... | collective-permute-start | bytes 983048 | tf_op jit(solution)/shard_map/ppermute | solution.py:228
  7.4 6.9 %collective-permute-done = bf16[128,1280]{1,0:T(8,128)(2,1)S(1)} collective-permute-done((bf16[128,1280]{1,0:T(8,128)(2,1)S(1)}, bf16[128,1280]{1,0:T(8,128)(2,1)S(1)}, u32[]{:S(2)}, u32[]{:S(2)}) %collective-permute-start) | collective-permute-done | bytes 327712 | tf_op jit(solution)/shard_map/ppermute | solution.py:228
  14.3 0.7 fusion.5
  15.0 0.6 slice.34.refs_8_
  15.7 17.5 %attention.1 = (bf16[16,64,640]{2,1,0:T(8,128)(2,1)}, bf16[16,64,640]{2,1,0:T(8,128)(2,1)}) custom-call(s32[1,4096]{1,0:T(1,128)} %refs_0_.1, bf16[512,4096]{1,0:T(8,128)(2,1)} %bitcast.28, bf16[512,4096]{1,0:T(8,128)(2,1)} %bitcast.29, bf16[512,512]{1,0:T(8,128)(2,1)} %bitcast.30, bf16[512,512]{1,0:T(8,128)(2,1)} %bitcast.31, bf16[512,256]{1,0:T(8,128)(2,1)} %bitcast.32, ...), custom_call_target="tpu_custom_call" | custom-call | tf_op jit(solution)/shard_map/attention/pallas_call | solution.py:195
  33.2 0.0 collective-permute-start.1
  33.2 3.2 %collective-permute-done.1 = bf16[16,64,640]{2,1,0:T(8,128)(2,1)S(1)} collective-permute-done((bf16[16,64,640]{2,1,0:T(8,128)(2,1)}, bf16[16,64,640]{2,1,0:T(8,128)(2,1)S(1)}, u32[]{:S(2)}, u32[]{:S(2)}) %collective-permute-start.1) | collective-permute-done | bytes 1310752 | tf_op jit(solution)/shard_map/ppermute | solution.py:204
  36.4 0.0 copy-start
  36.4 1.1 %copy-done = bf16[16,64,640]{2,1,0:T(8,128)(2,1)} copy-done((bf16[16,64,640]{2,1,0:T(8,128)(2,1)}, bf16[16,64,640]{2,1,0:T(8,128)(2,1)S(1)}, u32[]{:S(2)}) %copy-start) | copy-done | bytes 1310744
  37.5 2.0 %convert_add_fusion = f32[16,64,640]{2,1,0:T(8,128)S(1)} fusion(bf16[16,64,640]{2,1,0:T(8,128)(2,1)} %copy-done, bf16[16,64,640]{2,1,0:T(8,128)(2,1)} %get-tuple-element.4), kind=kLoop, calls=%fused_computation | loop fusion | flops 1966080 | bytes 5242880 | tf_op jit(solution)/shard_map/add | solution.py:237
  39.5 1.0 %fusion.2 = (bf16[4,64,640]{2,1,0:T(8,128)(2,1)}, bf16[4,64,640]{2,1,0:T(8,128)(2,1)}, bf16[4,64,640]{2,1,0:T(8,128)(2,1)}) fusion(f32[4,4,64,640]{3,2,1,0:T(8,128)S(1)} %bitcast.26, s32[]{:T(128)S(6)} %select_n.27, s32[]{:T(128)S(6)} %select_n.29, s32[]{:T(128)S(6)} %select_n.28), kind=kLoop, calls=%fused_computation.7 | loop fusion | bytes 1966092 | tf_op jit(solution)/shard_map/convert_element_type | solution.py:216
  40.5 2.5 %collective-permute-start.4 = (bf16[4,64,640]{2,1,0:T(8,128)(2,1)}, bf16[4,64,640]{2,1,0:T(8,128)(2,1)S(1)}, u32[]{:S(2)}, u32[]{:S(2)}) collective-permute-start(bf16[4,64,640]{2,1,0:T(8,128)(2,1)} %get-tuple-element.7), channel_id=1, source_target_pairs={{0,1},{1,0},{2,3},{3,2},{4,5},{5,4},{6,7},{7,6},{8,9},{9,8},{10,11... | collective-permute-start | bytes 983048 | tf_op jit(solution)/shard_map/ppermute | solution.py:204
  43.0 1.5 %collective-permute-start.3 = (bf16[4,64,640]{2,1,0:T(8,128)(2,1)}, bf16[4,64,640]{2,1,0:T(8,128)(2,1)S(1)}, u32[]{:S(2)}, u32[]{:S(2)}) collective-permute-start(bf16[4,64,640]{2,1,0:T(8,128)(2,1)} %get-tuple-element.8), channel_id=1, source_target_pairs={{0,16},{1,17},{2,18},{3,19},{4,20},{5,21},{6,22},{7,23},{8,24},{9,... | collective-permute-start | bytes 983048 | tf_op jit(solution)/shard_map/ppermute | solution.py:204
  44.5 0.0 collective-permute-start.2
  44.5 7.2 %collective-permute-done.4 = bf16[4,64,640]{2,1,0:T(8,128)(2,1)S(1)} collective-permute-done((bf16[4,64,640]{2,1,0:T(8,128)(2,1)}, bf16[4,64,640]{2,1,0:T(8,128)(2,1)S(1)}, u32[]{:S(2)}, u32[]{:S(2)}) %collective-permute-start.4) | collective-permute-done | bytes 327712 | tf_op jit(solution)/shard_map/ppermute | solution.py:204
  51.7 0.0 copy-start.1
  51.7 7.9 %collective-permute-done.3 = bf16[4,64,640]{2,1,0:T(8,128)(2,1)S(1)} collective-permute-done((bf16[4,64,640]{2,1,0:T(8,128)(2,1)}, bf16[4,64,640]{2,1,0:T(8,128)(2,1)S(1)}, u32[]{:S(2)}, u32[]{:S(2)}) %collective-permute-start.3) | collective-permute-done | bytes 327712 | tf_op jit(solution)/shard_map/ppermute | solution.py:204
  59.7 0.0 copy-done.1
  59.7 0.0 copy-start.2
  59.7 0.7 copy-done.2
  60.4 0.0 collective-permute-done.2
  60.4 1.3 %fusion.1 = f32[4,64,640]{2,1,0:T(8,128)S(1)} fusion(bf16[4,64,640]{2,1,0:T(8,128)(2,1)} %copy-done.1, bf16[4,64,640]{2,1,0:T(8,128)(2,1)} %copy-done.2, bf16[4,64,640]{2,1,0:T(8,128)(2,1)} %collective-permute-done.2, f32[4,4,64,640]{3,2,1,0:T(8,128)S(1)} %bitcast.27, s32[]{:T(128)S(6)} %select_n.26), kind=kLoop, calls=%fused_computation.3 | loop fusion | flops 983040 | bytes 2293764 | tf_op jit(solution)/shard_map/add | solution.py:217
  61.7 2.7 %collective-permute-start.7 = (bf16[1,64,640]{2,1,0:T(8,128)(2,1)S(1)}, bf16[1,64,640]{2,1,0:T(8,128)(2,1)S(1)}, u32[]{:S(2)}, u32[]{:S(2)}) collective-permute-start(bf16[1,64,640]{2,1,0:T(8,128)(2,1)S(1)} %get-tuple-element.10), channel_id=1, source_target_pairs={{0,4},{1,5},{2,6},{3,7},{4,0},{5,1},{6,2},{7,3},{8,12},{9,13},{10,... | collective-permute-start | bytes 245768 | tf_op jit(solution)/shard_map/ppermute | solution.py:204
  64.4 1.6 %collective-permute-start.6 = (bf16[1,64,640]{2,1,0:T(8,128)(2,1)S(1)}, bf16[1,64,640]{2,1,0:T(8,128)(2,1)S(1)}, u32[]{:S(2)}, u32[]{:S(2)}) collective-permute-start(bf16[1,64,640]{2,1,0:T(8,128)(2,1)S(1)} %get-tuple-element.11), channel_id=1, source_target_pairs={{0,2},{1,3},{2,0},{3,1},{4,6},{5,7},{6,4},{7,5},{8,10},{9,11},{10,... | collective-permute-start | bytes 245768 | tf_op jit(solution)/shard_map/ppermute | solution.py:204
  66.0 0.2 collective-permute-start.5
  66.2 2.2 %collective-permute-done.7 = bf16[1,64,640]{2,1,0:T(8,128)(2,1)S(1)} collective-permute-done((bf16[1,64,640]{2,1,0:T(8,128)(2,1)S(1)}, bf16[1,64,640]{2,1,0:T(8,128)(2,1)S(1)}, u32[]{:S(2)}, u32[]{:S(2)}) %collective-permute-start.7) | collective-permute-done | bytes 81952 | tf_op jit(solution)/shard_map/ppermute | solution.py:204
  68.4 0.5 collective-permute-done.6
  68.9 3.3 %collective-permute-done.5 = bf16[1,64,640]{2,1,0:T(8,128)(2,1)S(1)} collective-permute-done((bf16[1,64,640]{2,1,0:T(8,128)(2,1)S(1)}, bf16[1,64,640]{2,1,0:T(8,128)(2,1)S(1)}, u32[]{:S(2)}, u32[]{:S(2)}) %collective-permute-start.5) | collective-permute-done | bytes 81952 | tf_op jit(solution)/shard_map/ppermute | solution.py:204
  72.3 0.7 slice.35
  72.9 0.6 slice.36
  (3 shorter events, 0.1 us)
Async XLA Ops:
  2.5 11.8 %collective-permute-start = (bf16[128,1280]{1,0:T(8,128)(2,1)S(1)}, bf16[128,1280]{1,0:T(8,128)(2,1)S(1)}, u32[]{:S(2)}, u32[]{:S(2)}) collective-permute-start(bf16[128,1280]{1,0:T(8,128)(2,1)S(1)} %pad_maximum_fusion), channel_id=1, source_target_pairs={{0,1},{1,2},{2,3},{3,4},{4,5},{5,6},{6,7},{8,9},{9,10},{10,11},{11... | collective-permute-start | bytes 983048 | tf_op jit(solution)/shard_map/ppermute | solution.py:228
  33.2 3.2 %collective-permute-start.1 = (bf16[16,64,640]{2,1,0:T(8,128)(2,1)}, bf16[16,64,640]{2,1,0:T(8,128)(2,1)S(1)}, u32[]{:S(2)}, u32[]{:S(2)}) collective-permute-start(bf16[16,64,640]{2,1,0:T(8,128)(2,1)} %get-tuple-element.5), channel_id=1, source_target_pairs={{0,8},{1,9},{2,10},{3,11},{4,12},{5,13},{6,14},{7,15},{8,0},{9,1},... | collective-permute-start | bytes 3932168 | tf_op jit(solution)/shard_map/ppermute | solution.py:204
  36.4 1.1 %copy-start = (bf16[16,64,640]{2,1,0:T(8,128)(2,1)}, bf16[16,64,640]{2,1,0:T(8,128)(2,1)S(1)}, u32[]{:S(2)}) copy-start(bf16[16,64,640]{2,1,0:T(8,128)(2,1)S(1)} %collective-permute-done.1) | copy-start | bytes 3932164
  40.5 11.3 %collective-permute-start.4 = (bf16[4,64,640]{2,1,0:T(8,128)(2,1)}, bf16[4,64,640]{2,1,0:T(8,128)(2,1)S(1)}, u32[]{:S(2)}, u32[]{:S(2)}) collective-permute-start(bf16[4,64,640]{2,1,0:T(8,128)(2,1)} %get-tuple-element.7), channel_id=1, source_target_pairs={{0,1},{1,0},{2,3},{3,2},{4,5},{5,4},{6,7},{7,6},{8,9},{9,8},{10,11... | collective-permute-start | bytes 983048 | tf_op jit(solution)/shard_map/ppermute | solution.py:204
  43.0 16.7 %collective-permute-start.3 = (bf16[4,64,640]{2,1,0:T(8,128)(2,1)}, bf16[4,64,640]{2,1,0:T(8,128)(2,1)S(1)}, u32[]{:S(2)}, u32[]{:S(2)}) collective-permute-start(bf16[4,64,640]{2,1,0:T(8,128)(2,1)} %get-tuple-element.8), channel_id=1, source_target_pairs={{0,16},{1,17},{2,18},{3,19},{4,20},{5,21},{6,22},{7,23},{8,24},{9,... | collective-permute-start | bytes 983048 | tf_op jit(solution)/shard_map/ppermute | solution.py:204
  44.5 15.9 %collective-permute-start.2 = (bf16[4,64,640]{2,1,0:T(8,128)(2,1)}, bf16[4,64,640]{2,1,0:T(8,128)(2,1)}, u32[]{:S(2)}, u32[]{:S(2)}) collective-permute-start(bf16[4,64,640]{2,1,0:T(8,128)(2,1)} %get-tuple-element.6), channel_id=1, source_target_pairs={{0,17},{1,16},{2,19},{3,18},{4,21},{5,20},{6,23},{7,22},{8,25},{9,... | collective-permute-start | bytes 983048 | tf_op jit(solution)/shard_map/ppermute | solution.py:204
  51.7 7.9 %copy-start.1 = (bf16[4,64,640]{2,1,0:T(8,128)(2,1)}, bf16[4,64,640]{2,1,0:T(8,128)(2,1)S(1)}, u32[]{:S(2)}) copy-start(bf16[4,64,640]{2,1,0:T(8,128)(2,1)S(1)} %collective-permute-done.4) | copy-start | bytes 983044
  59.7 0.7 copy-start.2
  61.7 6.7 %collective-permute-start.7 = (bf16[1,64,640]{2,1,0:T(8,128)(2,1)S(1)}, bf16[1,64,640]{2,1,0:T(8,128)(2,1)S(1)}, u32[]{:S(2)}, u32[]{:S(2)}) collective-permute-start(bf16[1,64,640]{2,1,0:T(8,128)(2,1)S(1)} %get-tuple-element.10), channel_id=1, source_target_pairs={{0,4},{1,5},{2,6},{3,7},{4,0},{5,1},{6,2},{7,3},{8,12},{9,13},{10,... | collective-permute-start | bytes 245768 | tf_op jit(solution)/shard_map/ppermute | solution.py:204
  64.4 4.5 %collective-permute-start.6 = (bf16[1,64,640]{2,1,0:T(8,128)(2,1)S(1)}, bf16[1,64,640]{2,1,0:T(8,128)(2,1)S(1)}, u32[]{:S(2)}, u32[]{:S(2)}) collective-permute-start(bf16[1,64,640]{2,1,0:T(8,128)(2,1)S(1)} %get-tuple-element.11), channel_id=1, source_target_pairs={{0,2},{1,3},{2,0},{3,1},{4,6},{5,7},{6,4},{7,5},{8,10},{9,11},{10,... | collective-permute-start | bytes 245768 | tf_op jit(solution)/shard_map/ppermute | solution.py:204
  66.0 6.2 %collective-permute-start.5 = (bf16[1,64,640]{2,1,0:T(8,128)(2,1)S(1)}, bf16[1,64,640]{2,1,0:T(8,128)(2,1)S(1)}, u32[]{:S(2)}, u32[]{:S(2)}) collective-permute-start(bf16[1,64,640]{2,1,0:T(8,128)(2,1)S(1)} %get-tuple-element.9), channel_id=1, source_target_pairs={{0,6},{1,7},{2,4},{3,5},{4,2},{5,3},{6,0},{7,1},{8,14},{9,15},{10,... | collective-permute-start | bytes 245768 | tf_op jit(solution)/shard_map/ppermute | solution.py:204

commit v2 on v1

--- a/solution.py
+++ b/solution.py
@@ -36,11 +36,41 @@
     return at
 
 
-def attention_kernel(blocks, per, kv_heads, dp, seq, order, *refs):
-    seg_ref, q_ref, g_ref, k_ref, v_ref, pj_ref, hk_ref, hv_ref, hp_ref = refs[:9]
-    keep_ref, send_ref, bias, pt, kt, dqt, dk, dv = refs[9:]
-    B = hk_ref.shape[0]
-    own = q_ref.shape[0]
+def pack_kernel(k_ref, v_ref, pj_ref, out_ref):
+    kw = k_ref.shape[1]
+    out_ref[:, :kw] = k_ref[...]
+    out_ref[:, kw : 2 * kw] = v_ref[...]
+    out_ref[:, 2 * kw :] = pj_ref[...]
+
+
+def pack(keys, values, proj, B):
+    last = lambda i: (keys.shape[0] // B - 1, 0)
+    width = 2 * keys.shape[1] + proj.shape[1]
+    return pl.pallas_call(
+        pack_kernel,
+        grid=(1,),
+        in_specs=[pl.BlockSpec((B, a.shape[1]), last) for a in (keys, values, proj)],
+        out_specs=pl.BlockSpec((B, width), lambda i: (0, 0)),
+        out_shape=jax.ShapeDtypeStruct((B, width), keys.dtype),
+        name="pack",
+    )(keys, values, proj)
+
+
+def attention_kernel(plan, *refs):
+    steps, first, sizes, order = plan
+    kv_heads, dp, seq = sizes
+    seg_ref, q_ref, g_ref, k_ref, v_ref, pj_ref = refs[:6]
+    refs = refs[6:]
+    hk_ref = hv_ref = hp_ref = qa_ref = kva_ref = None
+    if not first:
+        hk_ref, hv_ref, hp_ref = refs[:3]
+        refs = refs[3:]
+        if len(refs) == 10:
+            qa_ref, kva_ref = refs[:2]
+            refs = refs[2:]
+    out_a, out_b, bias, pt, kt, dqt, dk, dv = refs
+    B = DOC
+    own, width = q_ref.shape
     nb = own // B
     R = pj_ref.shape[1]
     f32, bf = jnp.float32, jnp.bfloat16
@@ -52,13 +82,18 @@
     cur2 = jnp.concatenate([cur, cur], axis=1)
     group = pl.program_id(0)
     r = R // dp
+    blocks = sorted({n for n, _ in steps})
+    key_blocks = range(blocks[0], nb + 1)
+
+    def block_of(ref, halo, n):
+        return ref[(n - 1) * B : n * B] if n else halo[...]
 
     @pl.when(group == 0)
     def _():
         dev = lax.axis_index("seq")
         low = lax.axis_index("dp") % 2
-        for n in range(nb + 1):
-            rows = (hp_ref[...] if n == 0 else pj_ref[(n - 1) * B : n * B]).astype(f32).T
+        for n in key_blocks:
+            rows = block_of(pj_ref, hp_ref, n).astype(f32).T
             rows = rows.reshape(dp // 2, 2, r, B)
             for half in range(2):
                 part = jnp.where(low == half, rows[:, 0], rows[:, 1]).reshape(R // 2, B)
@@ -76,8 +111,8 @@
 
     dk[...] = jnp.zeros_like(dk)
     dv[...] = jnp.zeros_like(dv)
-    for n in range(nb + 1):
-        kt[n] = (hk_ref[...] if n == 0 else k_ref[(n - 1) * B : n * B]).T
+    for n in key_blocks:
+        kt[n] = block_of(k_ref, hk_ref, n).T
 
     def window(ref, halo, n):
         if n:
@@ -120,7 +155,6 @@
         for j, c in enumerate(cols(hp)):
             dqt[c, n * B : (n + 1) * B] = dq[:, j * B : (j + 1) * B]
 
-    steps = [(n, hp) for hp in range(per // 2) for n in blocks]
     ready = scores(*steps[0])
     done = None
     for i, step in enumerate(steps):
@@ -131,68 +165,100 @@
         ready = after
     gradients(*done)
 
-    def store(value, s, lane, width):
+    def store(value, s, lane, size):
         for row in range(dp // 2):
             at = place_of(row, s, order)
-            keep_ref[at, :, lane : lane + width] = value[row * r : (row + 1) * r]
-            send_ref[at, :, lane : lane + width] = value[R // 2 + row * r : R // 2 + (row + 1) * r]
-
-    lo, hi = blocks[0] * B, (blocks[-1] + 1) * B
+            out_a[at, :, lane : lane + size] = value[row * r : (row + 1) * r].astype(bf)
+            out_b[at, :, lane : lane + size] = value[R // 2 + row * r : R // 2 + (row + 1) * r].astype(bf)
+
+    per = width // HD
     q_width = per * kv_heads * HD // seq
     kv_width = 2 * kv_heads * HD // seq
-    tok = pt[:, lo + B : hi + B]
     wide = min(2 * HD, q_width)
-    for j in range(0, per * HD, wide):
-        value = (dot(tok, dqt[j : j + wide, lo:hi], NT) * scale).astype(bf)
-        store(value, group * (per * HD // q_width) + j // q_width, j % q_width, wide)
-    tok = pt[:, lo : hi + B]
+    for j in range(0, width, wide):
+        mine = sorted(n for n, hp in steps if hp == j // (2 * HD))
+        lo, hi = mine[0] * B, (mine[-1] + 1) * B
+        value = dot(pt[:, lo + B : hi + B], dqt[j : j + wide, lo:hi], NT) * scale
+        if first:
+            out_a[:, j : j + wide] = value.astype(out_a.dtype)
+            continue
+        if qa_ref is not None and j < qa_ref.shape[1]:
+            value = value + qa_ref[:, j : j + wide].astype(f32)
+        store(value, group * (width // q_width) + j // q_width, j % q_width, wide)
+    tok = pt[:, blocks[0] * B :]
     for which, ref in enumerate((dk, dv)):
-        value = dot(tok, ref[lo : hi + B].astype(bf), NN)
-        value = (value * scale if which == 0 else value).astype(bf)
+        value = dot(tok, ref[blocks[0] * B :].astype(bf), NN)
+        value = value * scale if which == 0 else value
+        if first:
+            out_b[:, which * HD : (which + 1) * HD] = value
+            continue
+        if kva_ref is not None:
+            value = value + kva_ref[:, which * HD : (which + 1) * HD]
         for j in range(0, HD, kv_width):
             s = which * (seq // 2) + group * (HD // kv_width) + j // kv_width
             store(value[:, j : j + kv_width], s, q_width, kv_width)
 
 
-def attention(blocks, kv_heads, dp, seq, order, queries, grad_out, keys, values, proj, halo, segments):
-    hk, hv, hp = halo
-    B = hk.shape[0]
+def attention(steps, sizes, order, queries, grad_out, keys, values, proj, segments, halo=None, before=()):
+    kv_heads, dp, seq = sizes
+    first = halo is None
+    B = DOC
     own, width = queries.shape
-    per = width // HD // kv_heads
+    cut = width // kv_heads // (2 if first else 1)
     nb = own // B
-    R = proj.shape[1]
-    pieces = dp // 2 * seq
-    piece = (pieces, R // dp, width // seq + 2 * kv_heads * HD // seq)
+    R, kw = proj.shape[1], keys.shape[1]
     bf, f32 = jnp.bfloat16, jnp.float32
     whole = lambda i: (0, 0)
     col = lambda i: (0, i)
+    heads = (lambda i: (0, 2 * i)) if first else col
+    in_specs = [
+        pl.BlockSpec(segments.shape, whole),
+        pl.BlockSpec((own, cut), heads),
+        pl.BlockSpec((own, cut), heads),
+        pl.BlockSpec((own, HD), col),
+        pl.BlockSpec((own, HD), col),
+        pl.BlockSpec((own, R), whole),
+    ]
+    args = [segments, queries, grad_out, keys, values, proj]
+    if first:
+        out_specs = [pl.BlockSpec((R, cut), col), pl.BlockSpec((R, 2 * HD), col)]
+        out_shape = [
+            jax.ShapeDtypeStruct((R, cut * kv_heads), bf),
+            jax.ShapeDtypeStruct((R, 2 * HD * kv_heads), f32),
+        ]
+    else:
+        in_specs += [
+            pl.BlockSpec((B, HD), col),
+            pl.BlockSpec((B, HD), lambda i: (0, kv_heads + i)),
+            pl.BlockSpec((B, R), lambda i: (0, 2 * kw // R)),
+        ]
+        args += [halo] * 3
+        piece = (dp // 2 * seq, R // dp, width // seq + 2 * kw // seq)
+        out_specs = [pl.BlockSpec(piece, lambda i: (0, 0, 0))] * 2
+        out_shape = [jax.ShapeDtypeStruct(piece, bf)] * 2
+        for a in before:
+            in_specs.append(pl.BlockSpec((R, a.shape[1] // kv_heads), col))
+            args.append(a)
     call = pl.pallas_call(
-        functools.partial(attention_kernel, blocks, per, kv_heads, dp, seq, order),
+        functools.partial(attention_kernel, (steps, first, sizes, order)),
         grid=(kv_heads,),
-        in_specs=[
-            pl.BlockSpec(segments.shape, whole),
-            pl.BlockSpec((own, per * HD), col),
-            pl.BlockSpec((own, per * HD), col),
-            pl.BlockSpec((own, HD), col),
-            pl.BlockSpec((own, HD), col),
-            pl.BlockSpec((own, R), whole),
-            pl.BlockSpec((B, HD), col),
-            pl.BlockSpec((B, HD), col),
-            pl.BlockSpec((B, R), whole),
-        ],
-        out_specs=[pl.BlockSpec(piece, lambda i: (0, 0, 0))] * 2,
-        out_shape=[jax.ShapeDtypeStruct(piece, bf)] * 2,
+        in_specs=in_specs,
+        out_specs=out_specs,
+        out_shape=out_shape,
         scratch_shapes=[
             pltpu.VMEM((nb, B, B), f32),
             pltpu.VMEM((R, own + B), bf),
             pltpu.VMEM((nb + 1, HD, B), bf),
-            pltpu.VMEM((per * HD, own), bf),
+            pltpu.VMEM((cut, own), bf),
             pltpu.VMEM((own + B, HD), f32),
             pltpu.VMEM((own + B, HD), f32),
         ],
-        name="attention",
+        cost_estimate=pl.CostEstimate(
+            flops=len(steps) * kv_heads * 100_000_000, bytes_accessed=own * cut * kv_heads * 4, transcendentals=0
+        ),
+        name="inner" if first else "attention",
     )
-    return call(segments, queries, grad_out, keys, values, proj, hk, hv, hp)
+    return call(*args)
 
 
 def exchange(value, dp, seq, flips):
@@ -204,18 +270,27 @@
     return lax.ppermute(value, ("dp", "seq"), pairs)
 
 
-def scatter_sum(value, dp, seq, bits):
-    f32, bf = jnp.float32, jnp.bfloat16
-    parts = value.reshape((1 << len(bits), -1) + value.shape[1:])
+def add_up(values):
+    total = values[0].astype(jnp.float32)
+    for value in values[1:]:
+        total = total + value.astype(jnp.float32)
+    return total
+
+
+def scatter_sum(values, dp, seq, bits):
     mine = 0
     for axis, b in bits:
         mine = mine * 2 + ((lax.axis_index(axis) >> b) & 1)
-    total = lax.dynamic_index_in_dim(parts, mine, 0, keepdims=False).astype(f32)
+
+    def part(i):
+        parts = [v.reshape((1 << len(bits), -1) + v.shape[1:]) for v in values]
+        return add_up([lax.dynamic_index_in_dim(v, i, 0, keepdims=False) for v in parts])
+
+    terms = []
     for flip in range((1 << len(bits)) - 1, 0, -1):
         flips = [bit for i, bit in enumerate(bits) if (flip >> (len(bits) - 1 - i)) & 1]
-        sent = lax.dynamic_index_in_dim(parts, mine ^ flip, 0, keepdims=False).astype(bf)
-        total = total + exchange(sent, dp, seq, flips).astype(f32)
-    return total
+        terms.append(exchange(part(mine ^ flip).astype(jnp.bfloat16), dp, seq, flips))
+    return [part(mine)] + terms
 
 
 def on_device(dp, seq, queries, keys, values, grad_out, proj_in, segments):
@@ -223,23 +298,21 @@
     kv_heads = keys.shape[2] // HD
     B = DOC
     nb = own // B
-    bf = jnp.bfloat16
-    tail = jnp.concatenate([keys[0, own - B :], values[0, own - B :], proj_in[0, own - B :]], axis=1)
-    tail = lax.ppermute(tail, "seq", [(i, i + 1) for i in range(seq - 1)])
-    kw = keys.shape[2]
-    halo = (tail[:, :kw], tail[:, kw : 2 * kw], tail[:, 2 * kw :])
+    pairs = queries.shape[2] // HD // kv_heads // 2
+    q, g, k, v, pj = (a[0] for a in (queries, grad_out, keys, values, proj_in))
+    halo = lax.ppermute(pack(k, v, pj, B), "seq", [(i, i + 1) for i in range(seq - 1)])
     stages = stage_bits(dp, seq)
     order = [bit for bits in stages[1:] for bit in bits]
-    keep, send = attention(
-        tuple(range(nb)), kv_heads, dp, seq, order,
-        queries[0], grad_out[0], keys[0], values[0], proj_in[0], halo, segments,
-    )
-    total = keep.astype(jnp.float32) + exchange(send, dp, seq, stages[0]).astype(jnp.float32)
+    sizes = (kv_heads, dp, seq)
+    early = [(n, hp) for hp in range(pairs // 2) for n in range(1, nb)]
+    late = [(n, hp) for hp in range(pairs) for n in range(nb) if (n, hp) not in early]
+    before = attention(early, sizes, order, q, g, k, v, pj, segments) if early else ()
+    keep, send = attention(late, sizes, order, q, g, k, v, pj, segments, halo, before)
+    terms = [keep, exchange(send, dp, seq, stages[0])]
     for bits in stages[1:]:
-        total = scatter_sum(total, dp, seq, bits)
-    total = total[0]
+        terms = scatter_sum(terms, dp, seq, bits)
     q_width = queries.shape[2] // seq
-    return total[:, :q_width], total[:, q_width:]
+    return add_up([t[0, :, :q_width] for t in terms]), add_up([t[0, :, q_width:] for t in terms])
 
 
 def solution(mesh):

time: 73.8 us -> 65.3 us (0.88)
  waiting for transfers between devices: 31.4 us -> 23.6 us
  local copies, waits for them, and re-layouts: 7.27 us -> 0.73 us
  Pallas kernels: 17.5 us -> 24 us
    ppermute x1, waiting for transfers between devices: 6.93 us -> 0.01 us  [on_device(): lax.ppermute(pack(k, v, pj, B), 'seq', [(i, i + 1) for i in range(seq - 1)])]
    pallas_call x1 -> x3, Pallas kernels: 17.5 us -> 24 us  [the longest x2 22.3 us: attention(): return call(*args)]
    slice x4 -> x0, local copies, waits for them, and re-layouts: 2.61 us -> none  [the longest x2 1.33 us: on_device(): halo = (tail[:, :kw], tail[:, kw:2 * kw], tail[:, 2 * kw:])]
    add x2, other arithmetic: 3.31 us -> 1.31 us  [add_up(): total = total + value.astype(jnp.float32)]
    squeeze x2 -> x0, local copies, waits for them, and re-layouts: 1.83 us -> none  [the longest x1 0.98 us: on_device(): values[0, own - B:]]
    convert_element_type x0 -> x2, other arithmetic: none -> 1.75 us  [scatter_sum(): part(mine ^ flip).astype(jnp.bfloat16)]
    unnamed x6 -> x2, local copies, waits for them, and re-layouts: 1.79 us -> 0.73 us
    convert_element_type x2 -> x0, local copies, waits for them, and re-layouts: 1.02 us -> none  [scatter_sum(): lax.dynamic_index_in_dim(parts, mine ^ flip, 0, keepdims=False).astype(bf)]
  transfers between devices with their start and end apart: 8 -> 8, of which waited for: 7 -> 7; matrix products, arithmetic and copies ran while one was open for 0% -> 0% of each run, Pallas kernels for 0% -> 14%
where the time goes in v2:
time: 65.3 us; the launch traced here: 65.1 us
  Pallas kernels  24 us (37%)
  waiting for transfers between devices  23.6 us (36%)
  starting transfers between devices  12.9 us (20%)
  other arithmetic  3.06 us (5%)
  local copies, waits for them, and re-layouts  0.73 us (1%)
  between operations  0.7 us (1%)
    ppermute x7, waiting for transfers between devices, exchange(): return lax.ppermute(value, ('dp', 'seq'), pairs)  23.6 us
    pallas_call x2, Pallas kernels, attention(): return call(*args)  22.3 us
    ppermute x7, starting transfers between devices, exchange(): return lax.ppermute(value, ('dp', 'seq'), pairs)  8.01 us
    ppermute x1, starting transfers between devices, on_device(): lax.ppermute(pack(k, v, pj, B), 'seq', [(i, i + 1) for i in range(seq - 1)])  4.88 us
    convert_element_type x2, other arithmetic, scatter_sum(): part(mine ^ flip).astype(jnp.bfloat16)  1.75 us
    pallas_call x1, Pallas kernels, pack(): pl.pallas_call(pack_kernel, grid=(1,), in_specs=[pl.BlockSpec((B, a.shape...  1.72 us
    add x2, other arithmetic, add_up(): total = total + value.astype(jnp.float32)  1.31 us
  transfers between devices with their start and end apart: 8, of which 7 were waited for; matrix products, arithmetic and copies ran while one was open for 0% of the time, Pallas kernels for 14%

profile of v2, /device:TPU:0, one launch (start us, length us, event | category | flops | bytes accessed | tf_op | source)
XLA Modules:
  0.0 65.1 jit_solution(9078287894231136235)
XLA Ops:
  0.6 1.7 %pack.1 = bf16[128,1280]{1,0:T(8,128)(2,1)} custom-call(bf16[512,512]{1,0:T(8,128)(2,1)} %bitcast.51, bf16[512,512]{1,0:T(8,128)(2,1)} %bitcast.54, bf16[512,256]{1,0:T(8,128)(2,1)} %bitcast.59), custom_call_target="tpu_custom_call" | custom-call | tf_op jit(solution)/shard_map/pack/pallas_call | solution.py:49
  2.3 4.9 %collective-permute-start = (bf16[128,1280]{1,0:T(8,128)(2,1)}, bf16[128,1280]{1,0:T(8,128)(2,1)S(1)}, u32[]{:S(2)}, u32[]{:S(2)}) collective-permute-start(bf16[128,1280]{1,0:T(8,128)(2,1)} %pack.1), channel_id=1, source_target_pairs={{0,1},{1,2},{2,3},{3,4},{4,5},{5,6},{6,7},{8,9},{9,10},{10,11},{11... | collective-permute-start | bytes 983048 | tf_op jit(solution)/shard_map/ppermute | solution.py:303
  7.2 9.1 %inner.1 = (bf16[256,2048]{1,0:T(8,128)(2,1)}, f32[256,1024]{1,0:T(8,128)}) custom-call(s32[1,4096]{1,0:T(1,128)} %refs_0_.3, bf16[512,4096]{1,0:T(8,128)(2,1)} %bitcast.47, bf16[512,4096]{1,0:T(8,128)(2,1)} %bitcast.49, bf16[512,512]{1,0:T(8,128)(2,1)} %bitcast.52, bf16[512,512]{1,0:T(8,128)(2,1)} %bitcast.55, bf16[512,256]{1,0:T(8,128)(2,1)} %bitcast.60), custom_call_target="tpu_custom_call" | custom-call | flops 2400000000 | bytes 4194304 | tf_op jit(solution)/shard_map/inner/pallas_call | solution.py:261
  16.3 0.0 collective-permute-done.refs_6_.refs_7_.refs_8_
  16.3 0.0 copy-start
  16.3 0.7 %copy-done = bf16[128,1280]{1,0:T(8,128)(2,1)} copy-done((bf16[128,1280]{1,0:T(8,128)(2,1)}, bf16[128,1280]{1,0:T(8,128)(2,1)S(1)}, u32[]{:S(2)}) %copy-start) | copy-done | bytes 327704
  17.0 13.3 %attention.1 = (bf16[16,64,640]{2,1,0:T(8,128)(2,1)}, bf16[16,64,640]{2,1,0:T(8,128)(2,1)}) custom-call(s32[1,4096]{1,0:T(1,128)} %refs_0_.3, bf16[512,4096]{1,0:T(8,128)(2,1)} %bitcast.48, bf16[512,4096]{1,0:T(8,128)(2,1)} %bitcast.50, bf16[512,512]{1,0:T(8,128)(2,1)} %bitcast.53, bf16[512,512]{1,0:T(8,128)(2,1)} %bitcast.56, bf16[512,256]{1,0:T(8,128)(2,1)} %bitcast.61, ...), custom_call_target="tpu_custom_call" | custom-call | flops 4000000000 | bytes 8388608 | tf_op jit(solution)/shard_map/attention/pallas_call | solution.py:261
  30.3 0.0 collective-permute-start.1
  30.3 3.2 %collective-permute-done.1 = bf16[16,64,640]{2,1,0:T(8,128)(2,1)S(1)} collective-permute-done((bf16[16,64,640]{2,1,0:T(8,128)(2,1)}, bf16[16,64,640]{2,1,0:T(8,128)(2,1)S(1)}, u32[]{:S(2)}, u32[]{:S(2)}) %collective-permute-start.1) | collective-permute-done | bytes 1310752 | tf_op jit(solution)/shard_map/ppermute | solution.py:270
  33.6 1.6 %fusion = (bf16[4,64,640]{2,1,0:T(8,128)(2,1)S(1)}, bf16[4,64,640]{2,1,0:T(8,128)(2,1)S(1)}, bf16[4,64,640]{2,1,0:T(8,128)(2,1)S(1)}, f32[1,4,64,640]{3,2,1,0:T(8,128)S(1)}) fusion(bf16[4,4,64,640]{3,2,1,0:T(8,128)(2,1)S(1)} %bitcast.58, s32[]{:T(128)S(6)} %select_n.45, bf16[4,4,64,640]{3,2,1,0:T(8,128)(2,1)} %bitcast.57, s32[]{:T(128)S(6)} %select_n.47, ...), kind=kLoop, calls=%fused_computation.4 | loop fusion | flops 2457600 | bytes 4259856 | tf_op jit(solution)/shard_map/convert_element_type | solution.py:292
  35.2 2.6 %collective-permute-start.2 = (bf16[4,64,640]{2,1,0:T(8,128)(2,1)S(1)}, bf16[4,64,640]{2,1,0:T(8,128)(2,1)S(1)}, u32[]{:S(2)}, u32[]{:S(2)}) collective-permute-start(bf16[4,64,640]{2,1,0:T(8,128)(2,1)S(1)} %get-tuple-element.10), channel_id=1, source_target_pairs={{0,17},{1,16},{2,19},{3,18},{4,21},{5,20},{6,23},{7,22},{8,25},{9,... | collective-permute-start | bytes 983048 | tf_op jit(solution)/shard_map/ppermute | solution.py:270
  37.7 0.5 collective-permute-start.3
  38.2 0.5 collective-permute-start.4
  38.7 8.0 %collective-permute-done.2 = bf16[4,64,640]{2,1,0:T(8,128)(2,1)S(1)} collective-permute-done((bf16[4,64,640]{2,1,0:T(8,128)(2,1)S(1)}, bf16[4,64,640]{2,1,0:T(8,128)(2,1)S(1)}, u32[]{:S(2)}, u32[]{:S(2)}) %collective-permute-start.2) | collective-permute-done | bytes 327712 | tf_op jit(solution)/shard_map/ppermute | solution.py:270
  46.8 6.1 %collective-permute-done.3 = bf16[4,64,640]{2,1,0:T(8,128)(2,1)S(1)} collective-permute-done((bf16[4,64,640]{2,1,0:T(8,128)(2,1)S(1)}, bf16[4,64,640]{2,1,0:T(8,128)(2,1)S(1)}, u32[]{:S(2)}, u32[]{:S(2)}) %collective-permute-start.3) | collective-permute-done | bytes 327712 | tf_op jit(solution)/shard_map/ppermute | solution.py:270
  52.9 0.1 collective-permute-done.4
  53.0 0.1 fusion.11
  53.2 3.7 %collective-permute-start.5 = (bf16[1,64,640]{2,1,0:T(8,128)(2,1)S(1)}, bf16[1,64,640]{2,1,0:T(8,128)(2,1)S(1)}, u32[]{:S(2)}, u32[]{:S(2)}) collective-permute-start(bf16[1,64,640]{2,1,0:T(8,128)(2,1)S(1)} %get-tuple-element.14), channel_id=1, source_target_pairs={{0,6},{1,7},{2,4},{3,5},{4,2},{5,3},{6,0},{7,1},{8,14},{9,15},{10,... | collective-permute-start | bytes 245768 | tf_op jit(solution)/shard_map/ppermute | solution.py:270
  56.8 0.0 collective-permute-start.6
  56.8 0.8 %collective-permute-start.7 = (bf16[1,64,640]{2,1,0:T(8,128)(2,1)S(1)}, bf16[1,64,640]{2,1,0:T(8,128)(2,1)S(1)}, u32[]{:S(2)}, u32[]{:S(2)}) collective-permute-start(bf16[1,64,640]{2,1,0:T(8,128)(2,1)S(1)} %get-tuple-element.15), channel_id=1, source_target_pairs={{0,4},{1,5},{2,6},{3,7},{4,0},{5,1},{6,2},{7,3},{8,12},{9,13},{10,... | collective-permute-start | bytes 245768 | tf_op jit(solution)/shard_map/ppermute | solution.py:270
  57.6 2.7 %collective-permute-done.5 = bf16[1,64,640]{2,1,0:T(8,128)(2,1)S(1)} collective-permute-done((bf16[1,64,640]{2,1,0:T(8,128)(2,1)S(1)}, bf16[1,64,640]{2,1,0:T(8,128)(2,1)S(1)}, u32[]{:S(2)}, u32[]{:S(2)}) %collective-permute-start.5) | collective-permute-done | bytes 81952 | tf_op jit(solution)/shard_map/ppermute | solution.py:270
  60.3 2.9 %collective-permute-done.6 = bf16[1,64,640]{2,1,0:T(8,128)(2,1)S(1)} collective-permute-done((bf16[1,64,640]{2,1,0:T(8,128)(2,1)S(1)}, bf16[1,64,640]{2,1,0:T(8,128)(2,1)S(1)}, u32[]{:S(2)}, u32[]{:S(2)}) %collective-permute-start.6) | collective-permute-done | bytes 81952 | tf_op jit(solution)/shard_map/ppermute | solution.py:270
  63.2 0.6 collective-permute-done.7
  63.8 0.6 fusion.19
  64.4 0.7 %fusion.16 = f32[64,512]{1,0:T(8,128)} fusion(f32[1,64,640]{2,1,0:T(8,128)S(1)} %get-tuple-element.17, bf16[1,64,640]{2,1,0:T(8,128)(2,1)S(1)} %collective-permute-done.7, bf16[1,64,640]{2,1,0:T(8,128)(2,1)S(1)} %collective-permute-done.6, bf16[1,64,640]{2,1,0:T(8,128)(2,1)S(1)} %collective-permute-done.5), kind=kLoop, calls=%fused_computation.25 | loop fusion | flops 196608 | bytes 458752 | tf_op jit(solution)/shard_map/add | solution.py:276
Async XLA Ops:
  2.3 14.0 %collective-permute-start = (bf16[128,1280]{1,0:T(8,128)(2,1)}, bf16[128,1280]{1,0:T(8,128)(2,1)S(1)}, u32[]{:S(2)}, u32[]{:S(2)}) collective-permute-start(bf16[128,1280]{1,0:T(8,128)(2,1)} %pack.1), channel_id=1, source_target_pairs={{0,1},{1,2},{2,3},{3,4},{4,5},{5,6},{6,7},{8,9},{9,10},{10,11},{11... | collective-permute-start | bytes 983048 | tf_op jit(solution)/shard_map/ppermute | solution.py:303
  16.3 0.7 %copy-start = (bf16[128,1280]{1,0:T(8,128)(2,1)}, bf16[128,1280]{1,0:T(8,128)(2,1)S(1)}, u32[]{:S(2)}) copy-start(bf16[128,1280]{1,0:T(8,128)(2,1)S(1)} %collective-permute-done.refs_6_.refs_7_.refs_8_) | copy-start | bytes 983044
  30.3 3.2 %collective-permute-start.1 = (bf16[16,64,640]{2,1,0:T(8,128)(2,1)}, bf16[16,64,640]{2,1,0:T(8,128)(2,1)S(1)}, u32[]{:S(2)}, u32[]{:S(2)}) collective-permute-start(bf16[16,64,640]{2,1,0:T(8,128)(2,1)} %get-tuple-element.9), channel_id=1, source_target_pairs={{0,8},{1,9},{2,10},{3,11},{4,12},{5,13},{6,14},{7,15},{8,0},{9,1},... | collective-permute-start | bytes 3932168 | tf_op jit(solution)/shard_map/ppermute | solution.py:270
  35.2 11.6 %collective-permute-start.2 = (bf16[4,64,640]{2,1,0:T(8,128)(2,1)S(1)}, bf16[4,64,640]{2,1,0:T(8,128)(2,1)S(1)}, u32[]{:S(2)}, u32[]{:S(2)}) collective-permute-start(bf16[4,64,640]{2,1,0:T(8,128)(2,1)S(1)} %get-tuple-element.10), channel_id=1, source_target_pairs={{0,17},{1,16},{2,19},{3,18},{4,21},{5,20},{6,23},{7,22},{8,25},{9,... | collective-permute-start | bytes 983048 | tf_op jit(solution)/shard_map/ppermute | solution.py:270
  37.7 15.2 %collective-permute-start.3 = (bf16[4,64,640]{2,1,0:T(8,128)(2,1)S(1)}, bf16[4,64,640]{2,1,0:T(8,128)(2,1)S(1)}, u32[]{:S(2)}, u32[]{:S(2)}) collective-permute-start(bf16[4,64,640]{2,1,0:T(8,128)(2,1)S(1)} %get-tuple-element.12), channel_id=1, source_target_pairs={{0,16},{1,17},{2,18},{3,19},{4,20},{5,21},{6,22},{7,23},{8,24},{9,... | collective-permute-start | bytes 983048 | tf_op jit(solution)/shard_map/ppermute | solution.py:270
  38.2 14.8 %collective-permute-start.4 = (bf16[4,64,640]{2,1,0:T(8,128)(2,1)S(1)}, bf16[4,64,640]{2,1,0:T(8,128)(2,1)S(1)}, u32[]{:S(2)}, u32[]{:S(2)}) collective-permute-start(bf16[4,64,640]{2,1,0:T(8,128)(2,1)S(1)} %get-tuple-element.11), channel_id=1, source_target_pairs={{0,1},{1,0},{2,3},{3,2},{4,5},{5,4},{6,7},{7,6},{8,9},{9,8},{10,11... | collective-permute-start | bytes 983048 | tf_op jit(solution)/shard_map/ppermute | solution.py:270
  53.2 7.1 %collective-permute-start.5 = (bf16[1,64,640]{2,1,0:T(8,128)(2,1)S(1)}, bf16[1,64,640]{2,1,0:T(8,128)(2,1)S(1)}, u32[]{:S(2)}, u32[]{:S(2)}) collective-permute-start(bf16[1,64,640]{2,1,0:T(8,128)(2,1)S(1)} %get-tuple-element.14), channel_id=1, source_target_pairs={{0,6},{1,7},{2,4},{3,5},{4,2},{5,3},{6,0},{7,1},{8,14},{9,15},{10,... | collective-permute-start | bytes 245768 | tf_op jit(solution)/shard_map/ppermute | solution.py:270
  56.8 6.3 %collective-permute-start.6 = (bf16[1,64,640]{2,1,0:T(8,128)(2,1)S(1)}, bf16[1,64,640]{2,1,0:T(8,128)(2,1)S(1)}, u32[]{:S(2)}, u32[]{:S(2)}) collective-permute-start(bf16[1,64,640]{2,1,0:T(8,128)(2,1)S(1)} %get-tuple-element.16), channel_id=1, source_target_pairs={{0,2},{1,3},{2,0},{3,1},{4,6},{5,7},{6,4},{7,5},{8,10},{9,11},{10,... | collective-permute-start | bytes 245768 | tf_op jit(solution)/shard_map/ppermute | solution.py:270
  56.8 6.9 %collective-permute-start.7 = (bf16[1,64,640]{2,1,0:T(8,128)(2,1)S(1)}, bf16[1,64,640]{2,1,0:T(8,128)(2,1)S(1)}, u32[]{:S(2)}, u32[]{:S(2)}) collective-permute-start(bf16[1,64,640]{2,1,0:T(8,128)(2,1)S(1)} %get-tuple-element.15), channel_id=1, source_target_pairs={{0,4},{1,5},{2,6},{3,7},{4,0},{5,1},{6,2},{7,3},{8,12},{9,13},{10,... | collective-permute-start | bytes 245768 | tf_op jit(solution)/shard_map/ppermute | solution.py:270
